TPU v7x, 512 devices: a whole 4x8x8 slice. The times are simulated.
512 devices in a mesh: img: 8 (over y_lo, core), cin: 8 (over x, y_hi), cout: 8 (over z).
Axes of the slice: x: 4, y: 8 (y_hi: 2, y_lo: 4; y = y_hi * 4 + y_lo), z: 8, core: 2. Of those that a mesh axis runs over, the one named last changes fastest.
Arguments:
- maps: bfloat16 [2, 8, 14, 14, 1024], P(None, 'img'), may hold values from -6 to 6
- w_first: bfloat16 [3, 3, 1024, 1024], P(None, None, 'cin', 'cout'), may hold values from -0.09375 to 0.09375
- w_reduce: bfloat16 [3, 3, 1024, 8192], P(None, None, 'img', ('cin', 'cout')), may hold values from -0.09375 to 0.09375
- w_wide: bfloat16 [3, 3, 8192, 8192], P(None, None, 'cin', ('img', 'cout')), may hold values from -0.03125 to 0.03125
Outputs:
- wide_out: bfloat16 [2, 8, 7, 7, 8192], P(None, 'cin', None, None, ('img', 'cout'))
All inputs are finite; a program needn't handle non-finite values.
Results may differ from a plain program's by a relative error of at most 0.014.
Values may be sent and summed in bfloat16 or wider, within the bound.
No kernel may reach another device: no remote copies, remote signals or barrier semaphores. Data moves between devices by JAX's collectives and lax.ppermute only.
A program may use at most 64 MiB of HBM per device.

v0:
```python
import jax
import jax.numpy as jnp
from jax import lax
from jax.sharding import PartitionSpec as P


def conv_block(padded, weight_flat, size, step):
    channels = padded.shape[3]
    windows = []
    for row_tap in range(3):
        for col_tap in range(3):
            windows.append(
                padded[
                    :,
                    row_tap : row_tap + step * (size - 1) + 1 : step,
                    col_tap : col_tap + step * (size - 1) + 1 : step,
                    :,
                ]
            )
    table = jnp.concatenate(windows, axis=3).reshape(-1, 9 * channels)
    total = jnp.dot(table, weight_flat, preferred_element_type=jnp.float32)
    return total.reshape(padded.shape[0], size, size, weight_flat.shape[1])


def conv_taps(padded, weight, size, step):
    count = padded.shape[0]
    channels = padded.shape[3]
    weight_flat = weight.reshape(9 * channels, weight.shape[3])
    group = 1
    for trial in range(1, 9):
        if count % trial == 0:
            group = trial
    blocks = padded.reshape(count // group, group, padded.shape[1], padded.shape[2], channels)
    results = lax.map(lambda block: conv_block(block, weight_flat, size, step), blocks)
    return results.reshape(count, size, size, weight.shape[3])


def pad_map(values):
    return jnp.pad(values, ((0, 0), (1, 1), (1, 1), (0, 0)))


def local(maps, w_first, w_reduce, w_wide):
    batches = maps.shape[0]
    side = maps.shape[2]
    half = side // 2
    in_block = w_first.shape[2]
    out_block = w_first.shape[3]
    flat = maps.reshape(-1, side, side, maps.shape[4])
    in_part = lax.dynamic_slice_in_dim(flat, lax.axis_index("cin") * in_block, in_block, 3)
    first_terms = conv_taps(pad_map(jnp.maximum(in_part, 0)), w_first, side, 1)
    first_terms = first_terms.reshape(batches, maps.shape[1], side, side, out_block)
    summed = lax.psum(first_terms, "cin")
    own_part = lax.dynamic_slice_in_dim(maps, lax.axis_index("cout") * out_block, out_block, 4)
    segment_maps = (own_part.astype(jnp.float32) + summed).astype(jnp.bfloat16)
    whole = lax.all_gather(segment_maps, "cout", axis=4, tiled=True)
    by_channel = lax.all_to_all(whole, "img", split_axis=4, concat_axis=1, tiled=True)
    images = by_channel.shape[1]
    rect_segment = jnp.maximum(by_channel, 0).reshape(-1, side, side, by_channel.shape[4])
    reduced = conv_taps(pad_map(rect_segment), w_reduce, half, 2).reshape(
        batches, images, half, half, w_reduce.shape[3]
    )
    out_width = w_wide.shape[3]
    summed_wide = lax.psum(reduced, "img")
    narrow = jnp.maximum(summed_wide, 0.0).astype(jnp.bfloat16)
    gathered = lax.all_gather(narrow, "cout", axis=4, tiled=True)
    flat_all = gathered.reshape(-1, half, half, gathered.shape[4])
    partial_value = conv_taps(pad_map(flat_all), w_wide, half, 1)
    partial_value = partial_value.reshape(batches, images, half, half, out_width)
    result = lax.psum_scatter(
        partial_value.astype(jnp.bfloat16), "cin", scatter_dimension=1, tiled=True
    )
    return result


def solution(mesh):
    in_specs = (
        P(None, "img", None, None, None),
        P(None, None, "cin", "cout"),
        P(None, None, "img", ("cin", "cout")),
        P(None, None, "cin", ("img", "cout")),
    )
    out_specs = P(None, "cin", None, None, ("img", "cout"))
    return jax.shard_map(local, mesh=mesh, in_specs=in_specs, out_specs=out_specs, check_vma=False)
```

profile of v0, /device:TPU:64, one launch (start us, length us, event | category | flops | bytes accessed | tf_op | source)
XLA Modules:
  0.0 461.7 jit_solution(14591765025077755233)
XLA Ops:
  9.3 116.6 %all-reduce.8.cloned.1.call-done = f32[2,1,14,14,128]{4,3,2,0,1:T(8,128)} async-done(((f32[2,1,14,14,128]{4,3,2,0,1:T(8,128)}), f32[2,1,14,14,128]{4,3,2,0,1:T(8,128)}) %all-reduce.8.cloned.1.call-update) | async-done | bytes 200720 | tf_op jit(solution)/shard_map/psum | solution.py:52
  126.9 26.5 %all_gather.6 = bf16[2,1,14,14,1024]{4,3,2,0,1:T(8,128)(2,1)S(1)} all-gather(bf16[2,1,14,14,128]{4,3,2,0,1:T(8,128)(2,1)S(1)} %add_convert_fusion), channel_id=1, replica_groups=mesh['img'=8,'cin'=8,'cout'=8] {'cout'}, dimensions={4}, use_global_device_ids=true | all-gather | bytes 903168 | tf_op jit(solution)/shard_map/all_gather | solution.py:55
  153.5 12.4 %copy.42 = bf16[2,1,14,14,1024]{3,0,2,1,4:T(2,128)(2,1)} copy(bf16[2,1,14,14,1024]{4,3,2,0,1:T(8,128)(2,1)S(1)} %all_gather.6) | data formatting | bytes 1605632 | tf_op jit(solution)/shard_map/all_gather | solution.py:55
  165.8 12.8 %reshape.68 = bf16[8,2,25088]{2,1,0:T(2,128)(2,1)} reshape(bf16[1024,1,14,2,14]{4,3,2,1,0:T(2,128)(2,1)} %bitcast.84) | data formatting | bytes 1605632
  178.7 3.5 all-to-all-start
  182.3 21.2 %all-to-all-done = bf16[8,2,25088]{2,1,0:T(2,128)(2,1)S(1)} async-done(((bf16[8,2,25088]{2,1,0:T(2,128)(2,1)}), bf16[8,2,25088]{2,1,0:T(2,128)(2,1)S(1)}, u32[]{:S(2)}, u32[]{:S(2)}) %all-to-all-start) | async-done | bytes 802848 | tf_op jit(solution)/shard_map/all_to_all | solution.py:56
  203.4 19.8 %reshape.69 = bf16[1024,1,14,2,14]{4,3,2,1,0:T(2,128)(2,1)} reshape(bf16[8,2,25088]{2,1,0:T(2,128)(2,1)S(1)} %all-to-all-done) | data formatting | bytes 1605632
  223.2 17.3 %copy.43 = bf16[2,1,14,14,1024]{4,0,3,2,1:T(2,128)(2,1)S(1)} copy(bf16[2,1,14,14,1024]{3,0,2,1,4:T(2,128)(2,1)} %bitcast.85) | data formatting | bytes 1605632 | tf_op jit(solution)/shard_map/all_to_all | solution.py:56
  241.7 1.2 pad_bitcast_fusion.1
  242.9 4.0 while.26
  242.9 1.2 dynamic-slice_bitcast_fusion.6
  246.9 31.9 %all-reduce.11 = bf16[2,8,7,7,128]{4,1,0,3,2:T(8,128)(2,1)S(1)} all-reduce(f32[2,8,7,7,128]{4,1,0,3,2:T(8,128)S(1)} %get-tuple-element.61), channel_id=1, replica_groups=mesh['img'=8,'cin'=8,'cout'=8] {'img'}, use_global_device_ids=true, to_apply=%region_3.4 | all-reduce | flops 100352 | bytes 602112 | tf_op jit(solution)/shard_map/psum | solution.py:63
  279.6 41.6 %all-gather.2.cloned.1.call-done = bf16[2,8,7,7,1024]{4,1,0,3,2:T(8,128)(2,1)} async-done(((bf16[2,8,7,7,128]{4,1,0,3,2:T(8,128)(2,1)}), bf16[2,8,7,7,1024]{4,1,0,3,2:T(8,128)(2,1)}) %all-gather.2.cloned.1.call-update) | async-done | bytes 1605648 | tf_op jit(solution)/shard_map/all_gather | solution.py:65
  321.2 3.3 pad_bitcast_fusion
  324.5 17.2 %while.27 = (s32[]{:T(128)}, bf16[2,8,7,7,128]{4,0,3,2,1:T(2,128)(2,1)S(1)}, bf16[2,8,9,9,1024]{4,1,0,3,2:T(8,128)(2,1)}, bf16[9216,128]{1,0:T(8,128)(2,1)S(1)}) while((s32[]{:T(128)}, bf16[2,8,7,7,128]{4,0,3,2,1:T(2,128)(2,1)S(1)}, bf16[2,8,9,9,1024]{4,1,0,3,2:T(8,128)(2,1)}, bf16[9216,128]{1,0:T(8,128)(2,1)S(1)}) %tuple.60), condition=%wide.region_5.6_spmd.clone, body=%wide.region_4.5_spmd.sunk.clone | while | flops 924844032 | bytes 27191356 | solution.py:34
  324.5 1.4 dynamic-slice_bitcast_fusion.7
  326.5 2.0 fusion.29
  328.7 4.4 dynamic_update_slice.16
  333.1 1.4 dynamic-slice_bitcast_fusion.7
  335.1 2.0 fusion.29
  337.3 4.4 dynamic_update_slice.16
  342.5 1.3 dynamic-slice.2
  343.7 109.5 %all-reduce.10.cloned.1.call-done = bf16[2,8,7,7,128]{4,0,3,2,1:T(2,128)(2,1)} async-done(((bf16[2,8,7,7,128]{4,0,3,2,1:T(2,128)(2,1)}), bf16[2,8,7,7,128]{4,0,3,2,1:T(2,128)(2,1)}) %all-reduce.10.cloned.1.call-update) | async-done | bytes 200720
  453.3 1.9 constant_dynamic-slice_fusion
  (73 shorter events, 10.3 us)
Async XLA Ops:
  6.5 1.6 copy-start
  6.5 119.4 %all-reduce.8.cloned.1.call-start = ((), (), s32[]{:S(2)}) async-start(), calls=%async_computation.1 | async-start | bytes 458752 | tf_op jit(solution)/shard_map/psum | solution.py:52
  178.7 24.8 %all-to-all-start = ((bf16[8,2,25088]{2,1,0:T(2,128)(2,1)}), bf16[8,2,25088]{2,1,0:T(2,128)(2,1)S(1)}, u32[]{:S(2)}, u32[]{:S(2)}) async-start(bf16[8,2,25088]{2,1,0:T(2,128)(2,1)} %reshape.68), calls=%async_computation | async-start | bytes 1605632 | tf_op jit(solution)/shard_map/all_to_all | solution.py:56
  182.2 139.0 %all-gather.2.cloned.1.call-start = ((), (), s32[]{:S(2)}) async-start(), calls=%async_computation.2 | async-start | bytes 1806336 | tf_op jit(solution)/shard_map/all_gather | solution.py:65
  223.2 19.7 %copy-start.2 = (bf16[3,3,128,128]{3,2,1,0:T(8,128)(2,1)S(1)}, bf16[3,3,128,128]{3,2,1,0:T(8,128)(2,1)}, u32[]{:S(2)}) copy-start(bf16[3,3,128,128]{3,2,1,0:T(8,128)(2,1)} %param.10) | copy-start | bytes 884740
  242.9 81.6 %copy-start.1 = (bf16[3,3,1024,128]{3,2,1,0:T(8,128)(2,1)S(1)}, bf16[3,3,1024,128]{3,2,1,0:T(8,128)(2,1)}, u32[]{:S(2)}) copy-start(bf16[3,3,1024,128]{3,2,1,0:T(8,128)(2,1)} %param.11) | copy-start | bytes 7077892
  279.5 173.7 %all-reduce.10.cloned.1.call-start = ((), (), s32[]{:S(2)}) async-start(), calls=%async_computation.3 | async-start | bytes 401408
  341.8 0.7 copy-start.3
Sparse Core Ops, SparseCore 0:
  10.3 115.6 all-reduce.7
  279.6 41.5 all-gather.1
  342.6 110.6 all-reduce.9
where the time goes:
time: 463 us; the launch traced here: 462 us
  waiting for transfers between devices  289 us (62%)
  local copies, waits for them, and re-layouts  88.5 us (19%)
  blocking collectives  58.4 us (13%)
  between operations  13.3 us (3%)
  matrix products  6.06 us (1%)
    psum x1, waiting for transfers between devices, local(): summed = lax.psum(first_terms, 'cin')  117 us
    unnamed x4, waiting for transfers between devices  110 us
    all_gather x1, waiting for transfers between devices, local(): gathered = lax.all_gather(narrow, 'cout', axis=4, tiled=True)  41.6 us
    unnamed x19, local copies, waits for them, and re-layouts  36.8 us
    psum x1, blocking collectives, local(): summed_wide = lax.psum(reduced, 'img')  31.9 us
    all_gather x1, blocking collectives, local(): whole = lax.all_gather(segment_maps, 'cout', axis=4, tiled=True)  26.5 us
    all_to_all x1, waiting for transfers between devices, local(): lax.all_to_all(whole, 'img', split_axis=4, concat_axis=1, tiled=True)  21.2 us
    all_to_all x1, local copies, waits for them, and re-layouts, local(): lax.all_to_all(whole, 'img', split_axis=4, concat_axis=1, tiled=True)  17.3 us
  transfers between devices with their start and end apart: 4, of which 4 were waited for; matrix products, arithmetic and copies ran while one was open for 0% of the time, Pallas kernels for 0%

commit v1 on v0

--- a/solution.py
+++ b/solution.py
@@ -53,7 +53,10 @@
     own_part = lax.dynamic_slice_in_dim(maps, lax.axis_index("cout") * out_block, out_block, 4)
     segment_maps = (own_part.astype(jnp.float32) + summed).astype(jnp.bfloat16)
     whole = lax.all_gather(segment_maps, "cout", axis=4, tiled=True)
-    by_channel = lax.all_to_all(whole, "img", split_axis=4, concat_axis=1, tiled=True)
+    by_channel = jnp.concatenate(
+        lax.all_to_all(jnp.stack(jnp.split(whole, lax.axis_size("img"), axis=4)), "img", 0, 0),
+        axis=1,
+    )
     images = by_channel.shape[1]
     rect_segment = jnp.maximum(by_channel, 0).reshape(-1, side, side, by_channel.shape[4])
     reduced = conv_taps(pad_map(rect_segment), w_reduce, half, 2).reshape(

time: 463 us -> 401 us (0.87)
  local copies, waits for them, and re-layouts: 88.5 us -> 27.6 us
    unnamed x19 -> x24, local copies, waits for them, and re-layouts: 36.8 us -> 4.5 us
    all_to_all x1 -> x0, local copies, waits for them, and re-layouts: 17.3 us -> none  [local(): lax.all_to_all(whole, 'img', split_axis=4, concat_axis=1, tiled=True)]
    all_gather x1 -> x0, local copies, waits for them, and re-layouts: 12.4 us -> none  [local(): whole = lax.all_gather(segment_maps, 'cout', axis=4, tiled=True)]
where the time goes in v1:
time: 401 us; the launch traced here: 400 us
  waiting for transfers between devices  289 us (72%)
  blocking collectives  58.4 us (15%)
  local copies, waits for them, and re-layouts  27.6 us (7%)
  between operations  13.2 us (3%)
  matrix products  6.06 us (2%)
    psum x1, waiting for transfers between devices, local(): summed = lax.psum(first_terms, 'cin')  117 us
    unnamed x4, waiting for transfers between devices  109 us
    all_gather x1, waiting for transfers between devices, local(): gathered = lax.all_gather(narrow, 'cout', axis=4, tiled=True)  41.6 us
    psum x1, blocking collectives, local(): summed_wide = lax.psum(reduced, 'img')  31.9 us
    all_gather x1, blocking collectives, local(): whole = lax.all_gather(segment_maps, 'cout', axis=4, tiled=True)  26.5 us
    all_to_all x1, waiting for transfers between devices, local(): lax.all_to_all(jnp.stack(jnp.split(whole, lax.axis_size('img'), axis=4)),...  21.2 us
    dynamic_update_slice x4, local copies, waits for them, and re-layouts, conv_taps(): lax.map(lambda block: conv_block(block, weight_flat, size, step), blocks)  9.11 us
  transfers between devices with their start and end apart: 4, of which 4 were waited for; matrix products, arithmetic and copies ran while one was open for 0% of the time, Pallas kernels for 0%

profile of v1, /device:TPU:64, one launch (start us, length us, event | category | flops | bytes accessed | tf_op | source)
XLA Modules:
  0.0 400.1 jit_solution(10652155590075912570)
XLA Ops:
  6.5 1.1 constant_dynamic-slice_fusion.2
  8.2 1.1 convolution_bitcast_fusion.1
  9.4 116.6 %all-reduce.8.cloned.1.call-done = f32[2,1,14,14,128]{4,3,2,0,1:T(8,128)} async-done(((f32[2,1,14,14,128]{4,3,2,0,1:T(8,128)}), f32[2,1,14,14,128]{4,3,2,0,1:T(8,128)}) %all-reduce.8.cloned.1.call-update) | async-done | bytes 200720 | tf_op jit(solution)/shard_map/psum | solution.py:52
  126.9 26.5 %all_gather.6 = bf16[2,1,14,14,1024]{4,3,2,0,1:T(8,128)(2,1)S(1)} all-gather(bf16[2,1,14,14,128]{4,3,2,0,1:T(8,128)(2,1)S(1)} %add_convert_fusion), channel_id=1, replica_groups=mesh['img'=8,'cin'=8,'cout'=8] {'cout'}, dimensions={4}, use_global_device_ids=true | all-gather | bytes 903168 | tf_op jit(solution)/shard_map/all_gather | solution.py:55
  153.8 1.5 copy.20
  155.3 3.5 all-to-all-start
  158.9 21.2 %all-to-all-done = bf16[8,2,1,14,14,128]{5,1,4,3,2,0:T(2,128)(2,1)S(1)} async-done(((bf16[8,2,1,14,14,128]{5,1,4,3,2,0:T(2,128)(2,1)}), bf16[8,2,1,14,14,128]{5,1,4,3,2,0:T(2,128)(2,1)S(1)}, u32[]{:S(2)}, u32[]{:S(2)}) %all-to-all-start) | async-done | bytes 802848 | tf_op jit(solution)/shard_map/all_to_all | solution.py:57
  180.2 1.2 pad_bitcast_fusion.1
  181.4 4.0 while.26
  181.4 1.2 dynamic-slice_bitcast_fusion.6
  183.5 1.1 dynamic-slice_bitcast_fusion.6
  185.4 31.9 %all-reduce.11 = bf16[2,8,7,7,128]{4,1,0,3,2:T(8,128)(2,1)S(1)} all-reduce(f32[2,8,7,7,128]{4,1,0,3,2:T(8,128)S(1)} %get-tuple-element.61), channel_id=1, replica_groups=mesh['img'=8,'cin'=8,'cout'=8] {'img'}, use_global_device_ids=true, to_apply=%region_3.4 | all-reduce | flops 100352 | bytes 602112 | tf_op jit(solution)/shard_map/psum | solution.py:66
  218.1 41.6 %all-gather.2.cloned.1.call-done = bf16[2,8,7,7,1024]{4,1,0,3,2:T(8,128)(2,1)} async-done(((bf16[2,8,7,7,128]{4,1,0,3,2:T(8,128)(2,1)}), bf16[2,8,7,7,1024]{4,1,0,3,2:T(8,128)(2,1)}) %all-gather.2.cloned.1.call-update) | async-done | bytes 1605648 | tf_op jit(solution)/shard_map/all_gather | solution.py:68
  259.7 3.3 pad_bitcast_fusion
  263.0 17.2 %while.27 = (s32[]{:T(128)}, bf16[2,8,7,7,128]{4,0,3,2,1:T(2,128)(2,1)S(1)}, bf16[2,8,9,9,1024]{4,1,0,3,2:T(8,128)(2,1)}, bf16[9216,128]{1,0:T(8,128)(2,1)S(1)}) while((s32[]{:T(128)}, bf16[2,8,7,7,128]{4,0,3,2,1:T(2,128)(2,1)S(1)}, bf16[2,8,9,9,1024]{4,1,0,3,2:T(8,128)(2,1)}, bf16[9216,128]{1,0:T(8,128)(2,1)S(1)}) %tuple.56), condition=%wide.region_5.6_spmd.clone, body=%wide.region_4.5_spmd.sunk.clone | while | flops 924844032 | bytes 27191356 | solution.py:34
  263.0 1.4 dynamic-slice_bitcast_fusion.7
  265.0 2.0 fusion.38
  267.2 4.4 %dynamic_update_slice.16 = bf16[2,8,7,7,128]{4,0,3,2,1:T(2,128)(2,1)S(1)} dynamic-update-slice(bf16[2,8,7,7,128]{4,0,3,2,1:T(2,128)(2,1)S(1)} %get-tuple-element.185, bf16[1,8,7,7,128]{4,0,3,2,1:T(2,128)(2,1)S(1)} %copy.53, s32[]{:T(128)} %get-tuple-element.184, s32[]{:T(128)} %constant.29.clone.1..sunk.1, s32[]{:T(128)} %constant.29.clone.1..sunk.1, s32[]{:T(128)} %constant.29.clone.1..sunk.1, ...) | dynamic-update-slice | bytes 200708 | tf_op jit(solution)/shard_map/while/body/jit(dynamic_update_index_in_dim)/dynamic_update_slice | solution.py:34
  271.6 1.4 dynamic-slice_bitcast_fusion.7
  273.6 2.0 fusion.38
  275.8 4.4 %dynamic_update_slice.16 = bf16[2,8,7,7,128]{4,0,3,2,1:T(2,128)(2,1)S(1)} dynamic-update-slice(bf16[2,8,7,7,128]{4,0,3,2,1:T(2,128)(2,1)S(1)} %get-tuple-element.185, bf16[1,8,7,7,128]{4,0,3,2,1:T(2,128)(2,1)S(1)} %copy.53, s32[]{:T(128)} %get-tuple-element.184, s32[]{:T(128)} %constant.29.clone.1..sunk.1, s32[]{:T(128)} %constant.29.clone.1..sunk.1, s32[]{:T(128)} %constant.29.clone.1..sunk.1, ...) | dynamic-update-slice | bytes 200708 | tf_op jit(solution)/shard_map/while/body/jit(dynamic_update_index_in_dim)/dynamic_update_slice | solution.py:34
  281.0 1.3 dynamic-slice.2
  282.2 109.4 %all-reduce.10.cloned.1.call-done = bf16[2,8,7,7,128]{4,0,3,2,1:T(2,128)(2,1)} async-done(((bf16[2,8,7,7,128]{4,0,3,2,1:T(2,128)(2,1)}), bf16[2,8,7,7,128]{4,0,3,2,1:T(2,128)(2,1)}) %all-reduce.10.cloned.1.call-update) | async-done | bytes 200720
  391.7 1.9 constant_dynamic-slice_fusion
  (77 shorter events, 6.2 us)
Async XLA Ops:
  6.5 1.7 copy-start
  6.5 119.4 %all-reduce.8.cloned.1.call-start = ((), (), s32[]{:S(2)}) async-start(), calls=%async_computation.1 | async-start | bytes 458752 | tf_op jit(solution)/shard_map/psum | solution.py:52
  6.5 174.9 %copy-start.2 = (bf16[3,3,128,128]{3,2,1,0:T(8,128)(2,1)S(1)}, bf16[3,3,128,128]{3,2,1,0:T(8,128)(2,1)}, u32[]{:S(2)}) copy-start(bf16[3,3,128,128]{3,2,1,0:T(8,128)(2,1)} %param.10) | copy-start | bytes 884740
  155.3 24.8 %all-to-all-start = ((bf16[8,2,1,14,14,128]{5,1,4,3,2,0:T(2,128)(2,1)}), bf16[8,2,1,14,14,128]{5,1,4,3,2,0:T(2,128)(2,1)S(1)}, u32[]{:S(2)}, u32[]{:S(2)}) async-start(bf16[8,2,1,14,14,128]{5,1,4,3,2,0:T(2,128)(2,1)} %copy.20), calls=%async_computation | async-start | bytes 1605632 | tf_op jit(solution)/shard_map/all_to_all | solution.py:57
  158.9 100.9 %all-gather.2.cloned.1.call-start = ((), (), s32[]{:S(2)}) async-start(), calls=%async_computation.2 | async-start | bytes 1806336 | tf_op jit(solution)/shard_map/all_gather | solution.py:68
  181.4 81.6 %copy-start.1 = (bf16[3,3,1024,128]{3,2,1,0:T(8,128)(2,1)S(1)}, bf16[3,3,1024,128]{3,2,1,0:T(8,128)(2,1)}, u32[]{:S(2)}) copy-start(bf16[3,3,1024,128]{3,2,1,0:T(8,128)(2,1)} %param.11) | copy-start | bytes 7077892
  218.0 173.6 %all-reduce.10.cloned.1.call-start = ((), (), s32[]{:S(2)}) async-start(), calls=%async_computation.3 | async-start | bytes 401408
  280.3 0.7 copy-start.3
Sparse Core Ops, SparseCore 0:
  10.3 115.6 all-reduce.7
  218.2 41.5 all-gather.1
  281.1 110.5 all-reduce.9
